TPU v7x, 32 devices: a whole 2x2x4 slice. The times are simulated.
32 devices in a mesh: row: 8 (over z, y), col: 4 (over x, core).
Axes of the slice: x: 2, y: 2, z: 4, core: 2. Of those that a mesh axis runs over, the one named last changes fastest.
Arguments:
- error: float32 [14336, 16384], P('row', 'col'), may hold values from -0.046875 to 0.046875
- covar: float32 [16384, 16384], P('row', 'col'), may hold values from -1 to 6, as said below
- basis: float32 [14336, 128], P('row'), may hold values from -6 to 6
Outputs:
- new_basis: float32 [14336, 128], P('row')
- factor: float32 [128, 128], replicated
Inputs may be any that keep to these rules, and one draw needn't show every extreme that they name: covar is symmetric and positive definite.
All inputs are finite; a program needn't handle non-finite values.
Results may differ from a plain program's by a relative error of at most 0.0001.
Values sent between devices are 32-bit elements; how exact they have to be, the bound alone decides.
A program may use at most 128 MiB of HBM per device.

v0:
```python
import jax
import jax.numpy as jnp
from jax import lax
from jax.sharding import PartitionSpec as P

ITERS = 2


def local(error, covar, basis):
    high = lax.Precision.HIGHEST
    col_width = error.shape[1]
    rows_all = error.shape[0] * lax.axis_size("row")
    current = basis
    lower = jnp.zeros((basis.shape[1], basis.shape[1]), jnp.float32)
    for step in range(ITERS):
        partial_proj = lax.dot_general(
            error,
            current,
            (((0,), (0,)), ((), ())),
            precision=high,
            preferred_element_type=jnp.float32,
        )
        projected = lax.psum(partial_proj, "row")
        image_part = jnp.dot(covar, projected, precision=high, preferred_element_type=jnp.float32)
        image_share = lax.psum_scatter(image_part, "col", scatter_dimension=0, tiled=True)
        whole = lax.all_gather(image_share, ("row", "col"), axis=0, tiled=True)
        needed = lax.dynamic_slice_in_dim(whole, lax.axis_index("col") * col_width, col_width, 0)
        block_part = jnp.dot(error, needed, precision=high, preferred_element_type=jnp.float32)
        block = lax.psum(block_part, "col")
        local_gram = jnp.dot(block.T, block, precision=high, preferred_element_type=jnp.float32)
        gram = lax.psum(local_gram, "row") / rows_all
        lower = jnp.linalg.cholesky(gram)
        current = lax.linalg.triangular_solve(
            lower, block, left_side=False, lower=True, transpose_a=True
        )
    return (current, lower.T)


def solution(mesh):
    in_specs = (P("row", "col"), P("row", "col"), P("row", None))
    out_specs = (P("row", None), P())
    return jax.shard_map(local, mesh=mesh, in_specs=in_specs, out_specs=out_specs, check_vma=False)
```

profile of v0, /device:TPU:0, one launch (start us, length us, event | category | flops | bytes accessed | tf_op | source)
XLA Modules:
  0.0 928.3 jit_solution(5317270569974142833)
XLA Ops:
  8.4 50.0 %fusion.13 = f32[4096,128]{1,0:T(8,128)} fusion(f32[1792,4096]{1,0:T(8,128)} %param.6, f32[1792,128]{1,0:T(8,128)S(1)} %copy-done), kind=kOutput, calls=%fused_computation.31 | convolution fusion | flops 11274289152 | bytes 32374784 | tf_op jit(solution)/shard_map/dot_general | solution.py:16
  58.4 105.1 %all-reduce.7.cloned.1.call-done = f32[4096,128]{1,0:T(8,128)} async-done(((f32[4096,128]{1,0:T(8,128)}), f32[4096,128]{1,0:T(8,128)}) %all-reduce.7.cloned.1.call-update) | async-done | bytes 2097168 | tf_op jit(solution)/shard_map/psum | solution.py:23
  163.5 42.7 %convolution_bitcast_fusion.2 = f32[2048,128]{0,1:T(8,128)} fusion(f32[4096,128]{1,0:T(8,128)} %all-reduce.7.cloned.1.call-done, f32[2048,4096]{1,0:T(8,128)} %param.7), kind=kOutput, calls=%fused_computation.2 | convolution fusion | flops 12884901888 | bytes 36700160 | tf_op jit(solution)/shard_map/dot_general | solution.py:24
  206.3 24.2 %reduce-scatter.3.cloned.1.call-done = f32[512,128]{0,1:T(8,128)} async-done(((f32[2048,128]{0,1:T(8,128)}), f32[512,128]{0,1:T(8,128)}) %reduce-scatter.3.cloned.1.call-update) | async-done | bytes 262160 | tf_op jit(solution)/shard_map/reduce_scatter | solution.py:25
  230.5 80.3 %all-gather.3.cloned.1.call-done = f32[16384,128]{0,1:T(8,128)} async-done(((f32[512,128]{0,1:T(8,128)}), f32[16384,128]{0,1:T(8,128)}) %all-gather.3.cloned.1.call-update) | async-done | bytes 8388624 | tf_op jit(solution)/shard_map/all_gather | solution.py:26
  310.8 34.1 %convolution_bitcast_fusion.6 = f32[1792,128]{0,1:T(8,128)} fusion(f32[1792,4096]{1,0:T(8,128)} %param.6, f32[16384,128]{0,1:T(8,128)} %all-gather.3.cloned.1.call-done, s32[]{:T(128)S(6)} %select_n.7), kind=kOutput, calls=%fused_computation.6 | convolution fusion | flops 11274289152 | bytes 32374788 | tf_op jit(solution)/shard_map/dot_general | solution.py:28
  345.1 35.2 %all-reduce.9.cloned.1.call-done = f32[1792,128]{0,1:T(8,128)} async-done(((f32[1792,128]{0,1:T(8,128)}), f32[1792,128]{0,1:T(8,128)}) %all-reduce.9.cloned.1.call-update) | async-done | bytes 917520 | tf_op jit(solution)/shard_map/psum | solution.py:29
  380.2 3.0 fusion.14
  383.3 70.2 %all-reduce.11.cloned.1.call-done = f32[128,128]{0,1:T(8,128)} async-done(((f32[128,128]{0,1:T(8,128)}), f32[128,128]{0,1:T(8,128)}) %all-reduce.11.cloned.1.call-update) | async-done | bytes 65552 | tf_op jit(solution)/shard_map/psum | solution.py:31
  455.3 11.7 %cholesky.44 = f32[128,128]{1,0:T(8,128)S(1)} custom-call(f32[128,128]{1,0:T(8,128)S(1)} %fusion.6), custom_call_target="Cholesky" | custom-call | tf_op jit(solution)/shard_map/jit(cholesky)/cholesky | solution.py:32
  468.3 9.8 %custom-call.6 = f32[1,128,128]{1,2,0:T(8,128)S(1)} custom-call(f32[1,128,128]{2,1,0:T(8,128)S(1)} %fusion.2), custom_call_target="InvertDiagBlocksLowerTriangular" | custom-call | tf_op jit(solution)/shard_map/triangular_solve/custom-call.0 | solution.py:33
  478.1 2.1 convolution_bitcast_fusion.4
  480.3 22.0 %convolution_bitcast_fusion = f32[4096,128]{0,1:T(8,128)} fusion(f32[1792,128]{0,1:T(8,128)S(1)} %convolution_bitcast_fusion.4, f32[1792,4096]{1,0:T(8,128)} %param.6), kind=kOutput, calls=%fused_computation | convolution fusion | flops 11274289152 | bytes 32374784 | tf_op jit(solution)/shard_map/dot_general | solution.py:16
  502.3 102.4 %all-reduce.13.cloned.1.call-done = f32[4096,128]{0,1:T(8,128)} async-done(((f32[4096,128]{0,1:T(8,128)}), f32[4096,128]{0,1:T(8,128)}) %all-reduce.13.cloned.1.call-update) | async-done | bytes 2097168 | tf_op jit(solution)/shard_map/psum | solution.py:23
  604.7 40.1 %convolution_bitcast_fusion.1 = f32[2048,128]{0,1:T(8,128)} fusion(f32[4096,128]{0,1:T(8,128)} %all-reduce.13.cloned.1.call-done, f32[2048,4096]{1,0:T(8,128)} %param.7), kind=kOutput, calls=%fused_computation.1 | convolution fusion | flops 12884901888 | bytes 36700160 | tf_op jit(solution)/shard_map/dot_general | solution.py:24
  644.8 24.2 %reduce-scatter.5.cloned.1.call-done = f32[512,128]{0,1:T(8,128)} async-done(((f32[2048,128]{0,1:T(8,128)}), f32[512,128]{0,1:T(8,128)}) %reduce-scatter.5.cloned.1.call-update) | async-done | bytes 262160 | tf_op jit(solution)/shard_map/reduce_scatter | solution.py:25
  669.1 80.3 %all-gather.5.cloned.1.call-done = f32[16384,128]{0,1:T(8,128)} async-done(((f32[512,128]{0,1:T(8,128)}), f32[16384,128]{0,1:T(8,128)}) %all-gather.5.cloned.1.call-update) | async-done | bytes 8388624 | tf_op jit(solution)/shard_map/all_gather | solution.py:26
  749.4 34.6 %convolution_bitcast_fusion.5 = f32[1792,128]{0,1:T(8,128)} fusion(f32[1792,4096]{1,0:T(8,128)} %param.6, f32[16384,128]{0,1:T(8,128)} %all-gather.5.cloned.1.call-done, s32[]{:T(128)S(6)} %select_n.7), kind=kOutput, calls=%fused_computation.5 | convolution fusion | flops 11274289152 | bytes 32374788 | tf_op jit(solution)/shard_map/dot_general | solution.py:28
  784.2 35.0 %all-reduce.15.cloned.1.call-done = f32[1792,128]{0,1:T(8,128)} async-done(((f32[1792,128]{0,1:T(8,128)}), f32[1792,128]{0,1:T(8,128)}) %all-reduce.15.cloned.1.call-update) | async-done | bytes 917520 | tf_op jit(solution)/shard_map/psum | solution.py:29
  819.3 3.0 fusion.15
  822.3 70.3 %all-reduce.17.cloned.1.call-done = f32[128,128]{0,1:T(8,128)} async-done(((f32[128,128]{0,1:T(8,128)}), f32[128,128]{0,1:T(8,128)}) %all-reduce.17.cloned.1.call-update) | async-done | bytes 65552 | tf_op jit(solution)/shard_map/psum | solution.py:31
  894.3 11.7 %cholesky.55 = f32[128,128]{1,0:T(8,128)S(1)} custom-call(f32[128,128]{1,0:T(8,128)S(1)} %fusion.4), custom_call_target="Cholesky" | custom-call | tf_op jit(solution)/shard_map/jit(cholesky)/cholesky | solution.py:32
  908.1 9.8 %custom-call.7 = f32[1,128,128]{1,2,0:T(8,128)S(1)} custom-call(f32[1,128,128]{2,1,0:T(8,128)S(1)} %get-tuple-element.7), custom_call_target="InvertDiagBlocksLowerTriangular" | custom-call | tf_op jit(solution)/shard_map/triangular_solve/custom-call.0 | solution.py:33
  917.9 2.1 convolution_bitcast_fusion.3
  (38 shorter events, 10.1 us)
Async XLA Ops:
  7.2 1.2 copy-start
  7.2 156.4 %all-reduce.7.cloned.1.call-start = ((), (), s32[]{:S(2)}) async-start(), calls=%async_computation.2 | async-start | bytes 4194304 | tf_op jit(solution)/shard_map/psum | solution.py:23
  58.4 172.1 %reduce-scatter.3.cloned.1.call-start = ((), (), s32[]{:S(2)}) async-start(), calls=%async_computation.3 | async-start | bytes 1310720 | tf_op jit(solution)/shard_map/reduce_scatter | solution.py:25
  206.2 104.6 %all-gather.3.cloned.1.call-start = ((), (), s32[]{:S(2)}) async-start(), calls=%async_computation.4 | async-start | bytes 8650752 | tf_op jit(solution)/shard_map/all_gather | solution.py:26
  230.5 149.7 %all-reduce.9.cloned.1.call-start = ((), (), s32[]{:S(2)}) async-start(), calls=%async_computation.5 | async-start | bytes 1835008 | tf_op jit(solution)/shard_map/psum | solution.py:29
  345.0 108.5 %all-reduce.11.cloned.1.call-start = ((), (), s32[]{:S(2)}) async-start(), calls=%async_computation.6 | async-start | bytes 131072 | tf_op jit(solution)/shard_map/psum | solution.py:31
  383.2 221.5 %all-reduce.13.cloned.1.call-start = ((), (), s32[]{:S(2)}) async-start(), calls=%async_computation.7 | async-start | bytes 4194304 | tf_op jit(solution)/shard_map/psum | solution.py:23
  502.3 166.7 %reduce-scatter.5.cloned.1.call-start = ((), (), s32[]{:S(2)}) async-start(), calls=%async_computation.8 | async-start | bytes 1310720 | tf_op jit(solution)/shard_map/reduce_scatter | solution.py:25
  644.8 104.6 %all-gather.5.cloned.1.call-start = ((), (), s32[]{:S(2)}) async-start(), calls=%async_computation.9 | async-start | bytes 8650752 | tf_op jit(solution)/shard_map/all_gather | solution.py:26
  669.0 150.2 %all-reduce.15.cloned.1.call-start = ((), (), s32[]{:S(2)}) async-start(), calls=%async_computation.10 | async-start | bytes 1835008 | tf_op jit(solution)/shard_map/psum | solution.py:29
  749.4 171.9 %copy-start.1 = (f32[1792,128]{1,0:T(8,128)S(1)}, f32[1792,128]{1,0:T(8,128)}, u32[]{:S(2)}) copy-start(f32[1792,128]{1,0:T(8,128)} %param.8) | copy-start | bytes 2752516
  784.0 108.5 %all-reduce.17.cloned.1.call-start = ((), (), s32[]{:S(2)}) async-start(), calls=%async_computation.11 | async-start | bytes 131072 | tf_op jit(solution)/shard_map/psum | solution.py:31
Sparse Core Ops, SparseCore 0:
  58.5 105.0 all-reduce.6
  206.4 24.0 reduce-scatter.2
  233.4 77.4 all-gather.2
  345.1 35.0 all-reduce.8
  384.0 69.3 all-reduce.10
  502.4 102.2 all-reduce.12
  644.9 24.0 reduce-scatter.4
  671.9 77.4 all-gather.4
  784.1 35.0 all-reduce.14
  823.1 69.3 all-reduce.16
where the time goes:
time: 937 us; the launch traced here: 928 us
  waiting for transfers between devices  627 us (67%)
  matrix products  234 us (25%)
  other arithmetic  49.1 us (5%)
  between operations  14.4 us (2%)
    psum x2, waiting for transfers between devices, local(): projected = lax.psum(partial_proj, 'row')  207 us
    all_gather x2, waiting for transfers between devices, local(): whole = lax.all_gather(image_share, ('row', 'col'), axis=0, tiled=True)  161 us
    psum x2, waiting for transfers between devices, local(): gram = lax.psum(local_gram, 'row') / rows_all  140 us
    dot_general x2, matrix products, local(): jnp.dot(covar, projected, precision=high, preferred_element_type=jnp.floa...  82.8 us
    dot_general x2, matrix products, local(): lax.dot_general(error, current, (((0,), (0,)), ((), ())), precision=high,...  71.9 us
    psum x2, waiting for transfers between devices, local(): block = lax.psum(block_part, 'col')  70.2 us
    dot_general x2, matrix products, local(): jnp.dot(error, needed, precision=high, preferred_element_type=jnp.float32)  68.7 us
    reduce_scatter x2, waiting for transfers between devices, local(): lax.psum_scatter(image_part, 'col', scatter_dimension=0, tiled=True)  48.3 us
  transfers between devices with their start and end apart: 10, of which 10 were waited for; matrix products, arithmetic and copies ran while one was open for 0% of the time, Pallas kernels for 0%

commit v1 on v0

--- a/solution.py
+++ b/solution.py
@@ -20,7 +20,7 @@
             precision=high,
             preferred_element_type=jnp.float32,
         )
-        projected = lax.psum(partial_proj, "row")
+        projected = jnp.sum(lax.all_gather(partial_proj, "row"), axis=0)
         image_part = jnp.dot(covar, projected, precision=high, preferred_element_type=jnp.float32)
         image_share = lax.psum_scatter(image_part, "col", scatter_dimension=0, tiled=True)
         whole = lax.all_gather(image_share, ("row", "col"), axis=0, tiled=True)

time: 937 us -> 1220 us (1.30)
  waiting for transfers between devices: 627 us -> 875 us
  local copies, waits for them, and re-layouts: 3.27 us -> 18.9 us
    all_gather x0 -> x2, waiting for transfers between devices: none -> 457 us  [local(): projected = jnp.sum(lax.all_gather(partial_proj, 'row'), axis=0)]
    psum x2 -> x0, waiting for transfers between devices: 207 us -> none  [local(): projected = lax.psum(partial_proj, 'row')]
    unnamed x6 -> x7, local copies, waits for them, and re-layouts: 3.09 us -> 18.7 us
where the time goes in v1:
time: 1220 us; the launch traced here: 1210 us
  waiting for transfers between devices  875 us (72%)
  matrix products  242 us (20%)
  other arithmetic  61.2 us (5%)
  local copies, waits for them, and re-layouts  18.9 us (2%)
  between operations  14.7 us (1%)
    all_gather x2, waiting for transfers between devices, local(): projected = jnp.sum(lax.all_gather(partial_proj, 'row'), axis=0)  457 us
    all_gather x2, waiting for transfers between devices, local(): whole = lax.all_gather(image_share, ('row', 'col'), axis=0, tiled=True)  161 us
    psum x2, waiting for transfers between devices, local(): gram = lax.psum(local_gram, 'row') / rows_all  140 us
    dot_general x2, matrix products, local(): jnp.dot(covar, projected, precision=high, preferred_element_type=jnp.floa...  90.6 us
    dot_general x2, matrix products, local(): lax.dot_general(error, current, (((0,), (0,)), ((), ())), precision=high,...  72.2 us
    psum x2, waiting for transfers between devices, local(): block = lax.psum(block_part, 'col')  70.2 us
    dot_general x2, matrix products, local(): jnp.dot(error, needed, precision=high, preferred_element_type=jnp.float32)  68.5 us
    reduce_scatter x2, waiting for transfers between devices, local(): lax.psum_scatter(image_part, 'col', scatter_dimension=0, tiled=True)  46.2 us
  transfers between devices with their start and end apart: 10, of which 10 were waited for; matrix products, arithmetic and copies ran while one was open for 0% of the time, Pallas kernels for 0%

profile of v1, /device:TPU:0, one launch (start us, length us, event | category | flops | bytes accessed | tf_op | source)
XLA Modules:
  0.0 1211.6 jit_solution(16127180276892198364)
XLA Ops:
  8.4 50.0 %fusion.13 = f32[4096,128]{1,0:T(8,128)} fusion(f32[1792,4096]{1,0:T(8,128)} %param.6, f32[1792,128]{1,0:T(8,128)S(1)} %copy-done), kind=kOutput, calls=%fused_computation.32 | convolution fusion | flops 11274289152 | bytes 32374784 | tf_op jit(solution)/shard_map/dot_general | solution.py:16
  58.4 230.1 %all-gather.11.cloned.1.call-done = f32[32768,128]{1,0:T(8,128)} async-done(((f32[4096,128]{1,0:T(8,128)}), f32[32768,128]{1,0:T(8,128)}) %all-gather.11.cloned.1.call-update) | async-done | bytes 16777232 | tf_op jit(solution)/shard_map/all_gather | solution.py:23
  288.5 6.8 reduce_sum.18
  295.3 51.8 %convolution_bitcast_fusion.2 = f32[2048,128]{0,1:T(8,128)} fusion(f32[4096,128]{1,0:T(8,128)S(1)} %reduce_sum.18, f32[2048,4096]{1,0:T(8,128)} %param.7), kind=kOutput, calls=%fused_computation.3 | convolution fusion | flops 12884901888 | bytes 36700160 | tf_op jit(solution)/shard_map/dot_general | solution.py:24
  347.2 23.1 %reduce-scatter.3.cloned.1.call-done = f32[512,128]{0,1:T(8,128)} async-done(((f32[2048,128]{0,1:T(8,128)}), f32[512,128]{0,1:T(8,128)}) %reduce-scatter.3.cloned.1.call-update) | async-done | bytes 262160 | tf_op jit(solution)/shard_map/reduce_scatter | solution.py:25
  370.4 80.3 %all-gather.7.cloned.1.call-done = f32[16384,128]{0,1:T(8,128)} async-done(((f32[512,128]{0,1:T(8,128)}), f32[16384,128]{0,1:T(8,128)}) %all-gather.7.cloned.1.call-update) | async-done | bytes 8388624 | tf_op jit(solution)/shard_map/all_gather | solution.py:26
  450.6 34.2 %convolution_bitcast_fusion.6 = f32[1792,128]{0,1:T(8,128)} fusion(f32[1792,4096]{1,0:T(8,128)} %param.6, f32[16384,128]{0,1:T(8,128)} %all-gather.7.cloned.1.call-done, s32[]{:T(128)S(6)} %select_n.7), kind=kOutput, calls=%fused_computation.7 | convolution fusion | flops 11274289152 | bytes 32374788 | tf_op jit(solution)/shard_map/dot_general | solution.py:28
  484.9 35.2 %all-reduce.5.cloned.1.call-done = f32[1792,128]{0,1:T(8,128)} async-done(((f32[1792,128]{0,1:T(8,128)}), f32[1792,128]{0,1:T(8,128)}) %all-reduce.5.cloned.1.call-update) | async-done | bytes 917520 | tf_op jit(solution)/shard_map/psum | solution.py:29
  523.1 70.2 %all-reduce.7.cloned.1.call-done = f32[128,128]{0,1:T(8,128)} async-done(((f32[128,128]{0,1:T(8,128)}), f32[128,128]{0,1:T(8,128)}) %all-reduce.7.cloned.1.call-update) | async-done | bytes 65552 | tf_op jit(solution)/shard_map/psum | solution.py:31
  595.1 11.7 cholesky.44
  608.2 9.8 custom-call.6
  620.1 22.2 %convolution_bitcast_fusion = f32[4096,128]{0,1:T(8,128)} fusion(f32[1792,128]{0,1:T(8,128)S(1)} %convolution_bitcast_fusion.4, f32[1792,4096]{1,0:T(8,128)} %param.6), kind=kOutput, calls=%fused_computation.1 | convolution fusion | flops 11274289152 | bytes 32374784 | tf_op jit(solution)/shard_map/dot_general | solution.py:16
  642.4 227.3 %all-gather.13.cloned.1.call-done = f32[32768,128]{0,1:T(8,128)} async-done(((f32[4096,128]{0,1:T(8,128)}), f32[32768,128]{0,1:T(8,128)}) %all-gather.13.cloned.1.call-update) | async-done | bytes 16777232 | tf_op jit(solution)/shard_map/all_gather | solution.py:23
  869.7 15.6 %copy.19 = f32[16,8,8,4096]{3,2,1,0:T(8,128)S(1)} copy(f32[16,8,8,4096]{3,1,2,0:T(8,128)} %bitcast.57) | data formatting | bytes 33554432
  885.3 5.3 bitcast_reduce_fusion
  890.6 38.8 %convolution_bitcast_fusion.1 = f32[2048,128]{0,1:T(8,128)} fusion(f32[4096,128]{0,1:T(8,128)S(1)} %bitcast_reduce_fusion, f32[2048,4096]{1,0:T(8,128)} %param.7), kind=kOutput, calls=%fused_computation.2 | convolution fusion | flops 12884901888 | bytes 36700160 | tf_op jit(solution)/shard_map/dot_general | solution.py:24
  929.5 23.1 %reduce-scatter.5.cloned.1.call-done = f32[512,128]{0,1:T(8,128)} async-done(((f32[2048,128]{0,1:T(8,128)}), f32[512,128]{0,1:T(8,128)}) %reduce-scatter.5.cloned.1.call-update) | async-done | bytes 262160 | tf_op jit(solution)/shard_map/reduce_scatter | solution.py:25
  952.7 80.3 %all-gather.9.cloned.1.call-done = f32[16384,128]{0,1:T(8,128)} async-done(((f32[512,128]{0,1:T(8,128)}), f32[16384,128]{0,1:T(8,128)}) %all-gather.9.cloned.1.call-update) | async-done | bytes 8388624 | tf_op jit(solution)/shard_map/all_gather | solution.py:26
  1032.9 34.3 %convolution_bitcast_fusion.5 = f32[1792,128]{0,1:T(8,128)} fusion(f32[1792,4096]{1,0:T(8,128)} %param.6, f32[16384,128]{0,1:T(8,128)} %all-gather.9.cloned.1.call-done, s32[]{:T(128)S(6)} %select_n.7), kind=kOutput, calls=%fused_computation.6 | convolution fusion | flops 11274289152 | bytes 32374788 | tf_op jit(solution)/shard_map/dot_general | solution.py:28
  1067.4 35.0 %all-reduce.9.cloned.1.call-done = f32[1792,128]{0,1:T(8,128)} async-done(((f32[1792,128]{0,1:T(8,128)}), f32[1792,128]{0,1:T(8,128)}) %all-reduce.9.cloned.1.call-update) | async-done | bytes 917520 | tf_op jit(solution)/shard_map/psum | solution.py:29
  1102.4 3.0 fusion.15
  1105.4 70.3 %all-reduce.11.cloned.1.call-done = f32[128,128]{0,1:T(8,128)} async-done(((f32[128,128]{0,1:T(8,128)}), f32[128,128]{0,1:T(8,128)}) %all-reduce.11.cloned.1.call-update) | async-done | bytes 65552 | tf_op jit(solution)/shard_map/psum | solution.py:31
  1177.5 11.7 cholesky.55
  1191.2 9.8 custom-call.7
  (41 shorter events, 17.1 us)
Async XLA Ops:
  7.2 1.2 copy-start
  7.2 281.3 %all-gather.11.cloned.1.call-start = ((), (), s32[]{:S(2)}) async-start(), calls=%async_computation.10 | async-start | bytes 18874368 | tf_op jit(solution)/shard_map/all_gather | solution.py:23
  58.4 311.9 %reduce-scatter.3.cloned.1.call-start = ((), (), s32[]{:S(2)}) async-start(), calls=%async_computation.2 | async-start | bytes 1310720 | tf_op jit(solution)/shard_map/reduce_scatter | solution.py:25
  347.2 103.5 %all-gather.7.cloned.1.call-start = ((), (), s32[]{:S(2)}) async-start(), calls=%async_computation.3 | async-start | bytes 8650752 | tf_op jit(solution)/shard_map/all_gather | solution.py:26
  370.3 149.7 %all-reduce.5.cloned.1.call-start = ((), (), s32[]{:S(2)}) async-start(), calls=%async_computation.4 | async-start | bytes 1835008 | tf_op jit(solution)/shard_map/psum | solution.py:29
  484.8 108.5 %all-reduce.7.cloned.1.call-start = ((), (), s32[]{:S(2)}) async-start(), calls=%async_computation.5 | async-start | bytes 131072 | tf_op jit(solution)/shard_map/psum | solution.py:31
  523.0 346.7 %all-gather.13.cloned.1.call-start = ((), (), s32[]{:S(2)}) async-start(), calls=%async_computation.11 | async-start | bytes 18874368 | tf_op jit(solution)/shard_map/all_gather | solution.py:23
  642.3 310.2 %reduce-scatter.5.cloned.1.call-start = ((), (), s32[]{:S(2)}) async-start(), calls=%async_computation.6 | async-start | bytes 1310720 | tf_op jit(solution)/shard_map/reduce_scatter | solution.py:25
  929.5 103.5 %all-gather.9.cloned.1.call-start = ((), (), s32[]{:S(2)}) async-start(), calls=%async_computation.7 | async-start | bytes 8650752 | tf_op jit(solution)/shard_map/all_gather | solution.py:26
  952.6 251.8 %copy-start.1 = (f32[1792,128]{1,0:T(8,128)S(1)}, f32[1792,128]{1,0:T(8,128)}, u32[]{:S(2)}) copy-start(f32[1792,128]{1,0:T(8,128)} %param.8) | copy-start | bytes 2752516
  952.6 149.8 %all-reduce.9.cloned.1.call-start = ((), (), s32[]{:S(2)}) async-start(), calls=%async_computation.8 | async-start | bytes 1835008 | tf_op jit(solution)/shard_map/psum | solution.py:29
  1067.3 108.3 %all-reduce.11.cloned.1.call-start = ((), (), s32[]{:S(2)}) async-start(), calls=%async_computation.9 | async-start | bytes 131072 | tf_op jit(solution)/shard_map/psum | solution.py:31
Sparse Core Ops, SparseCore 0:
  58.5 230.0 all-gather.10
  347.3 22.9 reduce-scatter.2
  373.2 77.3 all-gather.6
  484.9 35.0 all-reduce.4
  523.9 69.3 all-reduce.6
  642.5 227.1 all-gather.12
  929.6 22.9 reduce-scatter.4
  955.5 77.3 all-gather.8
  1067.4 34.9 all-reduce.8
  1106.2 69.3 all-reduce.10
